TPU v7x, 128 devices: a whole 4x4x4 slice. The times are simulated.
128 devices in a mesh: clip: 4 (over y_hi, core), ctx: 32 (over x, z, y_lo).
Axes of the slice: x: 4, y: 4 (y_hi: 2, y_lo: 2; y = y_hi * 2 + y_lo), z: 4, core: 2. Of those that a mesh axis runs over, the one named last changes fastest.
Arguments:
- queries: bfloat16 [16384, 4096], P(('clip', 'ctx')), parts along dimension 0, may hold values from -48 to 48
- key_rows: bfloat16 [16384, 4096], P(('clip', 'ctx')), parts along dimension 0, may hold values from -48 to 48
- values: bfloat16 [16384, 4096], P(('clip', 'ctx')), parts along dimension 0, may hold values from -6 to 6
- tangent_queries: bfloat16 [16384, 4096], P(('clip', 'ctx')), parts along dimension 0, may hold values from -6 to 6
- tangent_keys: bfloat16 [16384, 4096], P(('clip', 'ctx')), parts along dimension 0, may hold values from -6 to 6
- tangent_values: bfloat16 [16384, 4096], P(('clip', 'ctx')), parts along dimension 0, may hold values from -6 to 6
Outputs:
- attended: bfloat16 [16384, 4096], P(('clip', 'ctx')), parts along dimension 0
- tangent_output: bfloat16 [16384, 4096], P(('clip', 'ctx')), parts along dimension 0
There are 4 independent parts, one for each index of `clip`. A program takes and returns all parts, laid end to end along the dimension named above; each array names one. Nothing has to cross between parts.
All inputs are finite; a program needn't handle non-finite values.
Results may differ from a plain program's by a relative error of at most 0.012.
Values may be sent and summed in bfloat16 or wider, within the bound.
No kernel may reach another device: no remote copies, remote signals or barrier semaphores. Data moves between devices by JAX's collectives and lax.ppermute only.
A program may use at most 64 MiB of HBM per device.

v0:
```python
import jax
import jax.numpy as jnp
from jax import lax
from jax.sharding import PartitionSpec as P

HD = 128


def split_blocks(array, block):
    return array.reshape(array.shape[0] // block, block, array.shape[1], array.shape[2])


def probs_block(query_block, key_all, scale):
    scores = (
        jnp.einsum("qhd,khd->hqk", query_block, key_all, preferred_element_type=jnp.float32) * scale
    )
    top = jnp.max(scores, axis=-1, keepdims=True)
    raised = jnp.exp(scores - top)
    return raised / jnp.sum(raised, axis=-1, keepdims=True)


def primal_block(prob_half, value_all):
    return jnp.einsum("hqk,khd->qhd", prob_half, value_all, preferred_element_type=jnp.float32)


def tangent_block(
    query_block,
    tquery_block,
    probs,
    prob_half,
    key_all,
    value_all,
    tkey_all,
    tvalue_all,
    primal,
    scale,
):
    dscores = (
        jnp.einsum("qhd,khd->hqk", tquery_block, key_all, preferred_element_type=jnp.float32)
        + jnp.einsum("qhd,khd->hqk", query_block, tkey_all, preferred_element_type=jnp.float32)
    ) * scale
    weighted = probs * dscores
    correction = jnp.transpose(jnp.sum(weighted, axis=-1, keepdims=True), (1, 0, 2))
    weight_half = weighted.astype(jnp.bfloat16)
    return (
        jnp.einsum("hqk,khd->qhd", weight_half, value_all, preferred_element_type=jnp.float32)
        + jnp.einsum("hqk,khd->qhd", prob_half, tvalue_all, preferred_element_type=jnp.float32)
        - correction * primal
    )


def joined(blocks, total):
    return blocks.reshape(total, 1, blocks.shape[2], blocks.shape[3])


def joint_heads(pieces):
    query_all, key_all, value_all, tquery_all, tkey_all, tvalue_all = [
        piece[:, 0] for piece in pieces
    ]
    total = query_all.shape[0]
    block = min(512, total)
    scale = HD ** (-0.5)

    def one_block(pair):
        query_block, tquery_block = pair
        probs = probs_block(query_block, key_all, scale)
        prob_half = probs.astype(jnp.bfloat16)
        primal = primal_block(prob_half, value_all)
        tangent = tangent_block(
            query_block,
            tquery_block,
            probs,
            prob_half,
            key_all,
            value_all,
            tkey_all,
            tvalue_all,
            primal,
            scale,
        )
        return (primal.astype(jnp.bfloat16), tangent.astype(jnp.bfloat16))

    primal_blocks, tangent_blocks = lax.map(
        one_block, (split_blocks(query_all, block), split_blocks(tquery_all, block))
    )
    return (joined(primal_blocks, total), joined(tangent_blocks, total))


def body(queries, key_rows, values, tangent_queries, tangent_keys, tangent_values):
    groups = lax.axis_size("ctx")
    tok_rows = queries.shape[0]
    width = queries.shape[1]
    head_count = width // (groups * HD)

    def by_group(array):
        return array.reshape(tok_rows, groups, head_count, HD)

    out_half, tangent_half = joint_heads(
        (
            lax.all_to_all(by_group(queries), "ctx", split_axis=1, concat_axis=0, tiled=True),
            lax.all_to_all(by_group(key_rows), "ctx", split_axis=1, concat_axis=0, tiled=True),
            lax.all_to_all(by_group(values), "ctx", split_axis=1, concat_axis=0, tiled=True),
            lax.all_to_all(
                by_group(tangent_queries), "ctx", split_axis=1, concat_axis=0, tiled=True
            ),
            lax.all_to_all(by_group(tangent_keys), "ctx", split_axis=1, concat_axis=0, tiled=True),
            lax.all_to_all(
                by_group(tangent_values), "ctx", split_axis=1, concat_axis=0, tiled=True
            ),
        )
    )
    attended, tangent_output = (
        lax.all_to_all(out_half, "ctx", split_axis=0, concat_axis=1, tiled=True),
        lax.all_to_all(tangent_half, "ctx", split_axis=0, concat_axis=1, tiled=True),
    )
    return (attended.reshape(tok_rows, width), tangent_output.reshape(tok_rows, width))


def solution(mesh):
    return jax.shard_map(
        body,
        mesh=mesh,
        in_specs=(
            P(("clip", "ctx"), None),
            P(("clip", "ctx"), None),
            P(("clip", "ctx"), None),
            P(("clip", "ctx"), None),
            P(("clip", "ctx"), None),
            P(("clip", "ctx"), None),
        ),
        out_specs=(P(("clip", "ctx"), None), P(("clip", "ctx"), None)),
        check_vma=False,
    )
```

profile of v0, /device:TPU:0, one launch (start us, length us, event | category | flops | bytes accessed | tf_op | source)
XLA Modules:
  0.0 313.1 jit_solution(640032985709236972)
XLA Ops:
  0.6 2.4 copy.58
  3.0 9.3 %all-to-all-start = ((bf16[128,32,1,128]{0,3,2,1:T(8,128)(2,1)}), bf16[128,32,1,128]{0,3,2,1:T(8,128)(2,1)S(1)}, u32[]{:S(2)}, u32[]{:S(2)}) async-start(bf16[128,32,1,128]{0,3,2,1:T(8,128)(2,1)} %bitcast.16), calls=%async_computation | async-start | bytes 2097152 | tf_op jit(solution)/shard_map/all_to_all | solution.py:100
  12.3 2.3 copy.61
  14.6 15.2 %all-to-all-done = bf16[128,32,1,128]{0,3,2,1:T(8,128)(2,1)S(1)} async-done(((bf16[128,32,1,128]{0,3,2,1:T(8,128)(2,1)}), bf16[128,32,1,128]{0,3,2,1:T(8,128)(2,1)S(1)}, u32[]{:S(2)}, u32[]{:S(2)}) %all-to-all-start) | async-done | bytes 1048608 | tf_op jit(solution)/shard_map/all_to_all | solution.py:100
  29.8 4.1 %all-to-all-start.1 = ((bf16[128,32,1,128]{0,3,2,1:T(8,128)(2,1)}), bf16[128,32,1,128]{0,3,2,1:T(8,128)(2,1)S(1)}, u32[]{:S(2)}, u32[]{:S(2)}) async-start(bf16[128,32,1,128]{0,3,2,1:T(8,128)(2,1)} %bitcast.22), calls=%async_computation.1 | async-start | bytes 2097152 | tf_op jit(solution)/shard_map/all_to_all | solution.py:101
  35.2 15.8 %all-to-all-done.1 = bf16[128,32,1,128]{0,3,2,1:T(8,128)(2,1)S(1)} async-done(((bf16[128,32,1,128]{0,3,2,1:T(8,128)(2,1)}), bf16[128,32,1,128]{0,3,2,1:T(8,128)(2,1)S(1)}, u32[]{:S(2)}, u32[]{:S(2)}) %all-to-all-start.1) | async-done | bytes 1048608 | tf_op jit(solution)/shard_map/all_to_all | solution.py:101
  51.0 3.9 %all-to-all-start.2 = ((bf16[128,32,1,128]{0,3,2,1:T(8,128)(2,1)}), bf16[128,32,1,128]{0,3,2,1:T(8,128)(2,1)S(1)}, u32[]{:S(2)}, u32[]{:S(2)}) async-start(bf16[128,32,1,128]{0,3,2,1:T(8,128)(2,1)} %bitcast.157), calls=%async_computation.2 | async-start | bytes 2097152 | tf_op jit(solution)/shard_map/all_to_all | solution.py:102
  55.0 2.3 copy.67
  57.2 14.5 %all-to-all-done.2 = bf16[128,32,1,128]{0,3,2,1:T(8,128)(2,1)S(1)} async-done(((bf16[128,32,1,128]{0,3,2,1:T(8,128)(2,1)}), bf16[128,32,1,128]{0,3,2,1:T(8,128)(2,1)S(1)}, u32[]{:S(2)}, u32[]{:S(2)}) %all-to-all-start.2) | async-done | bytes 1048608 | tf_op jit(solution)/shard_map/all_to_all | solution.py:102
  71.8 4.7 %all-to-all-start.3 = ((bf16[128,32,1,128]{0,3,2,1:T(8,128)(2,1)}), bf16[128,32,1,128]{0,3,2,1:T(8,128)(2,1)}, u32[]{:S(2)}, u32[]{:S(2)}) async-start(bf16[128,32,1,128]{0,3,2,1:T(8,128)(2,1)} %bitcast.158), calls=%async_computation.3 | async-start | bytes 2097152 | tf_op jit(solution)/shard_map/all_to_all | solution.py:103
  76.4 2.3 copy.70
  78.7 13.6 %all-to-all-done.3 = bf16[128,32,1,128]{0,3,2,1:T(8,128)(2,1)} async-done(((bf16[128,32,1,128]{0,3,2,1:T(8,128)(2,1)}), bf16[128,32,1,128]{0,3,2,1:T(8,128)(2,1)}, u32[]{:S(2)}, u32[]{:S(2)}) %all-to-all-start.3) | async-done | bytes 1048608 | tf_op jit(solution)/shard_map/all_to_all | solution.py:103
  92.3 4.7 %all-to-all-start.4 = ((bf16[128,32,1,128]{0,3,2,1:T(8,128)(2,1)}), bf16[128,32,1,128]{0,3,2,1:T(8,128)(2,1)}, u32[]{:S(2)}, u32[]{:S(2)}) async-start(bf16[128,32,1,128]{0,3,2,1:T(8,128)(2,1)} %bitcast.159), calls=%async_computation.4 | async-start | bytes 2097152 | tf_op jit(solution)/shard_map/all_to_all | solution.py:106
  97.0 2.3 copy.73
  99.3 13.2 %all-to-all-done.4 = bf16[128,32,1,128]{0,3,2,1:T(8,128)(2,1)} async-done(((bf16[128,32,1,128]{0,3,2,1:T(8,128)(2,1)}), bf16[128,32,1,128]{0,3,2,1:T(8,128)(2,1)}, u32[]{:S(2)}, u32[]{:S(2)}) %all-to-all-start.4) | async-done | bytes 1048608 | tf_op jit(solution)/shard_map/all_to_all | solution.py:106
  112.4 4.8 %all-to-all-start.5 = ((bf16[128,32,1,128]{0,3,2,1:T(8,128)(2,1)}), bf16[128,32,1,128]{0,3,2,1:T(8,128)(2,1)}, u32[]{:S(2)}, u32[]{:S(2)}) async-start(bf16[128,32,1,128]{0,3,2,1:T(8,128)(2,1)} %bitcast.156), calls=%async_computation.5 | async-start | bytes 2097152 | tf_op jit(solution)/shard_map/all_to_all | solution.py:107
  120.0 2.3 copy.69
  123.9 9.0 %all-to-all-done.5 = bf16[128,32,1,128]{0,3,2,1:T(8,128)(2,1)} async-done(((bf16[128,32,1,128]{0,3,2,1:T(8,128)(2,1)}), bf16[128,32,1,128]{0,3,2,1:T(8,128)(2,1)}, u32[]{:S(2)}, u32[]{:S(2)}) %all-to-all-start.5) | async-done | bytes 1048608 | tf_op jit(solution)/shard_map/all_to_all | solution.py:107
  132.9 2.3 copy.75
  135.1 127.8 %while.12 = (s32[]{:T(128)}, bf16[8,512,1,128]{3,1,2,0:T(8,128)(2,1)}, bf16[8,512,1,128]{3,1,2,0:T(8,128)(2,1)}, bf16[8,512,1,128]{3,1,2,0:T(8,128)(2,1)}, bf16[...) while((s32[]{:T(128)}, ...), condition=%wide.region_4.5_spmd, body=%wide.region_0.4_spmd.sunk | while | flops 3253008896 | bytes 96092800 | solution.py:83
  135.1 2.2 multiply_reduce_fusion.2
  138.9 2.0 fusion.67
  140.9 2.2 fusion.68
  143.0 3.0 fusion.69
  149.2 1.9 fusion.71
  151.1 2.2 multiply_reduce_fusion.2
  154.9 2.0 fusion.67
  156.8 2.2 fusion.68
  159.0 3.0 fusion.69
  165.2 1.9 fusion.71
  167.1 2.2 multiply_reduce_fusion.2
  170.8 2.0 fusion.67
  172.8 2.2 fusion.68
  175.0 3.0 fusion.69
  181.1 1.9 fusion.71
  183.1 2.2 multiply_reduce_fusion.2
  186.8 2.0 fusion.67
  188.8 2.2 fusion.68
  191.0 3.0 fusion.69
  197.1 1.9 fusion.71
  199.0 2.2 multiply_reduce_fusion.2
  202.8 2.0 fusion.67
  204.8 2.2 fusion.68
  206.9 3.0 fusion.69
  213.1 1.9 fusion.71
  215.0 2.2 multiply_reduce_fusion.2
  218.8 2.0 fusion.67
  220.7 2.2 fusion.68
  222.9 3.0 fusion.69
  231.0 2.2 multiply_reduce_fusion.2
  234.7 2.0 fusion.67
  236.7 2.2 fusion.68
  238.9 3.0 fusion.69
  247.0 2.2 multiply_reduce_fusion.2
  250.7 2.0 fusion.67
  252.7 2.2 fusion.68
  254.9 3.0 fusion.69
  263.4 2.6 reduce.6
  267.1 4.2 %all-to-all-start.6 = ((bf16[32,2,8192]{2,1,0:T(2,128)(2,1)}), bf16[32,2,8192]{2,1,0:T(2,128)(2,1)S(1)}, u32[]{:S(2)}, u32[]{:S(2)}) async-start(bf16[32,2,8192]{2,1,0:T(2,128)(2,1)} %reshape.113), calls=%async_computation.6 | async-start | bytes 2097152 | tf_op jit(solution)/shard_map/all_to_all | solution.py:113
  271.3 2.6 reduce.7
  275.1 11.7 %all-to-all-done.6 = bf16[32,2,8192]{2,1,0:T(2,128)(2,1)S(1)} async-done(((bf16[32,2,8192]{2,1,0:T(2,128)(2,1)}), bf16[32,2,8192]{2,1,0:T(2,128)(2,1)S(1)}, u32[]{:S(2)}, u32[]{:S(2)}) %all-to-all-start.6) | async-done | bytes 1048608 | tf_op jit(solution)/shard_map/all_to_all | solution.py:113
  286.8 4.7 %all-to-all-start.7 = ((bf16[32,2,8192]{2,1,0:T(2,128)(2,1)}), bf16[32,2,8192]{2,1,0:T(2,128)(2,1)}, u32[]{:S(2)}, u32[]{:S(2)}) async-start(bf16[32,2,8192]{2,1,0:T(2,128)(2,1)} %reshape.115), calls=%async_computation.7 | async-start | bytes 2097152 | tf_op jit(solution)/shard_map/all_to_all | solution.py:114
  294.6 12.1 %all-to-all-done.7 = bf16[32,2,8192]{2,1,0:T(2,128)(2,1)} async-done(((bf16[32,2,8192]{2,1,0:T(2,128)(2,1)}), bf16[32,2,8192]{2,1,0:T(2,128)(2,1)}, u32[]{:S(2)}, u32[]{:S(2)}) %all-to-all-start.7) | async-done | bytes 1048608 | tf_op jit(solution)/shard_map/all_to_all | solution.py:114
  306.7 4.3 %reshape.116 = bf16[4096,1,1,128]{3,2,1,0:T(2,128)(2,1)S(1)} reshape(bf16[32,2,8192]{2,1,0:T(2,128)(2,1)} %all-to-all-done.7) | data formatting | bytes 2097152
  (62 shorter events, 56.8 us)
Async XLA Ops:
  0.6 33.2 %copy-start.1 = (bf16[128,4096]{1,0:T(8,128)(2,1)S(1)}, bf16[128,4096]{1,0:T(8,128)(2,1)}, u32[]{:S(2)}) copy-start(bf16[128,4096]{1,0:T(8,128)(2,1)} %param.10) | copy-start | bytes 3145732
  3.0 26.8 %all-to-all-start = ((bf16[128,32,1,128]{0,3,2,1:T(8,128)(2,1)}), bf16[128,32,1,128]{0,3,2,1:T(8,128)(2,1)S(1)}, u32[]{:S(2)}, u32[]{:S(2)}) async-start(bf16[128,32,1,128]{0,3,2,1:T(8,128)(2,1)} %bitcast.16), calls=%async_computation | async-start | bytes 2097152 | tf_op jit(solution)/shard_map/all_to_all | solution.py:100
  29.8 21.2 %all-to-all-start.1 = ((bf16[128,32,1,128]{0,3,2,1:T(8,128)(2,1)}), bf16[128,32,1,128]{0,3,2,1:T(8,128)(2,1)S(1)}, u32[]{:S(2)}, u32[]{:S(2)}) async-start(bf16[128,32,1,128]{0,3,2,1:T(8,128)(2,1)} %bitcast.22), calls=%async_computation.1 | async-start | bytes 2097152 | tf_op jit(solution)/shard_map/all_to_all | solution.py:101
  51.0 20.8 %all-to-all-start.2 = ((bf16[128,32,1,128]{0,3,2,1:T(8,128)(2,1)}), bf16[128,32,1,128]{0,3,2,1:T(8,128)(2,1)S(1)}, u32[]{:S(2)}, u32[]{:S(2)}) async-start(bf16[128,32,1,128]{0,3,2,1:T(8,128)(2,1)} %bitcast.157), calls=%async_computation.2 | async-start | bytes 2097152 | tf_op jit(solution)/shard_map/all_to_all | solution.py:102
  71.8 20.5 %all-to-all-start.3 = ((bf16[128,32,1,128]{0,3,2,1:T(8,128)(2,1)}), bf16[128,32,1,128]{0,3,2,1:T(8,128)(2,1)}, u32[]{:S(2)}, u32[]{:S(2)}) async-start(bf16[128,32,1,128]{0,3,2,1:T(8,128)(2,1)} %bitcast.158), calls=%async_computation.3 | async-start | bytes 2097152 | tf_op jit(solution)/shard_map/all_to_all | solution.py:103
  92.3 20.1 %all-to-all-start.4 = ((bf16[128,32,1,128]{0,3,2,1:T(8,128)(2,1)}), bf16[128,32,1,128]{0,3,2,1:T(8,128)(2,1)}, u32[]{:S(2)}, u32[]{:S(2)}) async-start(bf16[128,32,1,128]{0,3,2,1:T(8,128)(2,1)} %bitcast.159), calls=%async_computation.4 | async-start | bytes 2097152 | tf_op jit(solution)/shard_map/all_to_all | solution.py:106
  112.4 20.4 %all-to-all-start.5 = ((bf16[128,32,1,128]{0,3,2,1:T(8,128)(2,1)}), bf16[128,32,1,128]{0,3,2,1:T(8,128)(2,1)}, u32[]{:S(2)}, u32[]{:S(2)}) async-start(bf16[128,32,1,128]{0,3,2,1:T(8,128)(2,1)} %bitcast.156), calls=%async_computation.5 | async-start | bytes 2097152 | tf_op jit(solution)/shard_map/all_to_all | solution.py:107
  147.3 1.9 copy-start
  163.2 1.9 copy-start
  179.2 1.9 copy-start
  195.2 1.9 copy-start
  211.2 1.9 copy-start
  227.1 1.9 copy-start
  243.1 1.9 copy-start
  259.1 1.9 copy-start
  267.1 19.6 %all-to-all-start.6 = ((bf16[32,2,8192]{2,1,0:T(2,128)(2,1)}), bf16[32,2,8192]{2,1,0:T(2,128)(2,1)S(1)}, u32[]{:S(2)}, u32[]{:S(2)}) async-start(bf16[32,2,8192]{2,1,0:T(2,128)(2,1)} %reshape.113), calls=%async_computation.6 | async-start | bytes 2097152 | tf_op jit(solution)/shard_map/all_to_all | solution.py:113
  286.8 19.9 %all-to-all-start.7 = ((bf16[32,2,8192]{2,1,0:T(2,128)(2,1)}), bf16[32,2,8192]{2,1,0:T(2,128)(2,1)}, u32[]{:S(2)}, u32[]{:S(2)}) async-start(bf16[32,2,8192]{2,1,0:T(2,128)(2,1)} %reshape.115), calls=%async_computation.7 | async-start | bytes 2097152 | tf_op jit(solution)/shard_map/all_to_all | solution.py:114
where the time goes:
time: 315 us; the launch traced here: 313 us
  waiting for transfers between devices  105 us (33%)
  matrix products  99.6 us (32%)
  starting transfers between devices  40.3 us (13%)
  local copies, waits for them, and re-layouts  33.9 us (11%)
  other arithmetic  33 us (10%)
    dot_general x8, matrix products, tangent_block(): jnp.einsum('qhd,khd->hqk', query_block, tkey_all, preferred_element_type=...  23.7 us
    unnamed x16, local copies, waits for them, and re-layouts  23.3 us
    dot_general x8, matrix products, probs_block(): jnp.einsum('qhd,khd->hqk', query_block, key_all, preferred_element_type=j...  17.9 us
    dot_general x8, matrix products, tangent_block(): jnp.einsum('qhd,khd->hqk', tquery_block, key_all, preferred_element_type=...  17.3 us
    all_to_all x1, waiting for transfers between devices, body(): lax.all_to_all(by_group(key_rows), 'ctx', split_axis=1, concat_axis=0, ti...  15.8 us
    div x8, other arithmetic, probs_block(): return raised / jnp.sum(raised, axis=-1, keepdims=True)  15.8 us
    dot_general x8, matrix products, tangent_block(): jnp.einsum('hqk,khd->qhd', prob_half, tvalue_all, preferred_element_type=...  15.4 us
    dot_general x8, matrix products, primal_block(): jnp.einsum('hqk,khd->qhd', prob_half, value_all, preferred_element_type=j...  15.3 us
  transfers between devices with their start and end apart: 8, of which 8 were waited for; matrix products, arithmetic and copies ran while one was open for 8% of the time, Pallas kernels for 0%

commit v1 on v0

v1 whole, which is shorter than its diff:
```python
import functools

import jax
import jax.numpy as jnp
from jax import lax
from jax.experimental import pallas as pl
from jax.experimental.pallas import tpu as pltpu
from jax.sharding import PartitionSpec as P

HD = 128
PAIR = 2 * HD
SCALE = HD**-0.5
TO_LOG2 = 1.4426950408889634 * SCALE
CONTRACT_LAST = (((1,), (1,)), ((), ()))
BF16 = jnp.bfloat16
F32 = jnp.float32
VMEM_BYTES = 56 * 2**20


def dot_last(a, b):
    return lax.dot_general(a, b, CONTRACT_LAST, preferred_element_type=F32)


def dot(a, b):
    return jnp.dot(a, b, preferred_element_type=F32)


def pack_kernel(pairs, heads, *refs):
    ins, out = refs[:-1], refs[-1]
    row = 0
    for which, (start, count) in enumerate(pairs):
        left, right = ins[2 * which], ins[2 * which + 1]
        for h in range(heads):
            cols = slice(h * HD, (h + 1) * HD)
            out[h, row : row + count, :HD] = left[start : start + count, cols]
            out[h, row : row + count, HD:] = right[start : start + count, cols]
        row += count


def pack(arrays, pairs, heads=4):
    tokens, width = arrays[0].shape
    groups = width // HD
    rows = sum(count for _, count in pairs)
    return pl.pallas_call(
        functools.partial(pack_kernel, pairs, heads),
        grid=(groups // heads,),
        in_specs=[pl.BlockSpec((tokens, heads * HD), lambda i: (0, i))] * len(arrays),
        out_specs=pl.BlockSpec((heads, rows, PAIR), lambda i: (i, 0, 0)),
        out_shape=jax.ShapeDtypeStruct((groups, rows, PAIR), BF16),
        cost_estimate=pl.CostEstimate(
            flops=0, bytes_accessed=4 * groups * rows * PAIR, transcendentals=0
        ),
        name="pack",
    )(*arrays)


def unpack_kernel(heads, count, *refs):
    parts, (left, right) = refs[:count], refs[count:]
    row = 0
    for part in parts:
        rows = part.shape[1]
        for h in range(heads):
            cols = slice(h * HD, (h + 1) * HD)
            left[row : row + rows, cols] = part[h, :, :HD]
            right[row : row + rows, cols] = part[h, :, HD:]
        row += rows


def unpack(parts, heads=4):
    groups = parts[0].shape[0]
    tokens = sum(part.shape[1] for part in parts)
    out = jax.ShapeDtypeStruct((tokens, groups * HD), BF16)
    return pl.pallas_call(
        functools.partial(unpack_kernel, heads, len(parts)),
        grid=(groups // heads,),
        in_specs=[
            pl.BlockSpec((heads, part.shape[1], PAIR), lambda i: (i, 0, 0)) for part in parts
        ],
        out_specs=[pl.BlockSpec((tokens, heads * HD), lambda i: (0, i))] * 2,
        out_shape=[out, out],
        cost_estimate=pl.CostEstimate(
            flops=0, bytes_accessed=8 * tokens * groups * HD, transcendentals=0
        ),
        name="unpack",
    )(*parts)


def attend(tqq, keys, vals, twice, ones, scores, chunk, before):
    block, total = tqq.shape[0], keys.shape[0]
    scaled = tqq[:, HD:].astype(F32) * TO_LOG2
    high = scaled.astype(BF16)
    low = (scaled - high.astype(F32)).astype(BF16)
    query = jnp.concatenate([high, low], axis=1)
    top = jnp.full((block, HD), -jnp.inf, F32) if before is None else before[0]
    for start in range(0, total, chunk):
        part = dot_last(query, twice[start : start + chunk, :])
        scores[:, start : start + chunk] = part
        for c in range(0, chunk, HD):
            top = jnp.maximum(top, part[:, c : c + HD])
    top = jnp.broadcast_to(jnp.max(top, axis=1, keepdims=True), (block, HD))
    if before is None:
        norm = jnp.zeros((block, HD), F32)
        both = jnp.zeros((block, PAIR), F32)
        tangent = jnp.zeros((block, PAIR), F32)
    else:
        decay = jnp.exp2(before[0] - top)
        wide = jnp.concatenate([decay, decay], axis=1)
        norm, both, tangent = before[1] * decay, before[2] * wide, before[3] * wide
    shift = top[:, :1]
    for start in range(0, total, chunk):
        rows = slice(start, start + chunk)
        raised = jnp.exp2(scores[:, rows] - shift)
        for c in range(0, chunk, HD):
            norm = norm + raised[:, c : c + HD]
        weighted = (raised * dot_last(tqq, keys[rows, :])).astype(BF16)
        both = both + dot(raised.astype(BF16), vals[rows, :])
        tangent = tangent + dot(weighted, ones[rows, :])
    return top, norm, both, tangent


def prepare(kv_ref, twice, ones, keys, vals):
    @pl.when(pl.program_id(0) == 0)
    def _():
        total = keys.shape[0]
        rows = kv_ref.shape[1] // 2
        both = kv_ref[:, :rows, :].reshape(total, PAIR)
        keys[...] = both
        twice[:, :HD] = both[:, :HD]
        twice[:, HD:] = both[:, :HD]
        both = kv_ref[:, rows:, :].reshape(total, PAIR)
        vals[...] = both
        ones[:, :HD] = both[:, :HD]
        ones[:, HD:] = jnp.ones((total, HD), BF16)


def first_kernel(chunk, q_ref, kv_ref, *refs):
    (top, norm, both, tangent), (scores, twice, ones, keys, vals) = refs[:4], refs[4:]
    prepare(kv_ref, twice, ones, keys, vals)
    tqq = q_ref[...].reshape(scores.shape[0], PAIR)
    top[...], norm[...], both[...], tangent[...] = attend(
        tqq, keys, vals, twice, ones, scores, chunk, None
    )


def last_kernel(chunk, q_ref, kv_ref, top, norm, both, tangent, out, scores, twice, ones, keys, vals):
    prepare(kv_ref, twice, ones, keys, vals)
    tqq = q_ref[...].reshape(scores.shape[0], PAIR)
    before = (top[...], norm[...], both[...], tangent[...])
    _, total, pair, weighted = attend(tqq, keys, vals, twice, ones, scores, chunk, before)
    share = 1.0 / jnp.sum(total, axis=1, keepdims=True)
    primal = pair[:, :HD] * share
    scaled = weighted * (share * SCALE)
    moved = scaled[:, :HD] + pair[:, HD:] * share - scaled[:, HD:] * primal
    out[:, :, :HD] = primal.astype(BF16).reshape(out.shape[0], out.shape[1], HD)
    out[:, :, HD:] = moved.astype(BF16).reshape(out.shape[0], out.shape[1], HD)


def cost(queries, keys):
    return pl.CostEstimate(
        flops=16 * queries * keys * HD, bytes_accessed=8 * queries * PAIR, transcendentals=queries * keys
    )


def call(kernel, name, received, kv, kv_rows, kv_at, q_at, q_rows, state, first_block, chunk):
    groups = received.shape[0]
    rows = 16
    block = groups * rows
    steps = q_rows // rows
    total = groups * kv_rows
    state_specs = [
        pl.BlockSpec((block, width), lambda i: (i + first_block, 0))
        for width in (HD, HD, PAIR, PAIR)
    ]
    if state is None:
        out_specs = state_specs
        out_shape = [
            jax.ShapeDtypeStruct((steps * block, width), F32) for width in (HD, HD, PAIR, PAIR)
        ]
        state, in_state = (), []
    else:
        out_specs = pl.BlockSpec((groups, rows, PAIR), lambda i: (0, i, 0))
        out_shape = jax.ShapeDtypeStruct((groups, q_rows, PAIR), BF16)
        in_state = state_specs
    return pl.pallas_call(
        functools.partial(kernel, chunk),
        grid=(steps,),
        in_specs=[
            pl.BlockSpec((groups, rows, PAIR), lambda i: (0, i + q_at // rows, 0)),
            pl.BlockSpec((groups, 2 * kv_rows, PAIR), lambda i: (0, kv_at // (2 * kv_rows), 0)),
            *in_state,
        ],
        out_specs=out_specs,
        out_shape=out_shape,
        scratch_shapes=[
            pltpu.VMEM((block, total), F32),
            pltpu.VMEM((total, PAIR), BF16),
            pltpu.VMEM((total, PAIR), BF16),
            pltpu.VMEM((total, PAIR), BF16),
            pltpu.VMEM((total, PAIR), BF16),
        ],
        compiler_params=pltpu.CompilerParams(vmem_limit_bytes=VMEM_BYTES),
        cost_estimate=cost(steps * block, total),
        name=name,
    )(received, kv, *state)


def exchange(array):
    return lax.all_to_all(array, "ctx", split_axis=0, concat_axis=0, tiled=True)


def body(queries, key_rows, values, tangent_queries, tangent_keys, tangent_values):
    tokens = queries.shape[0]
    half = tokens // 2
    kv = (key_rows, tangent_keys, values, tangent_values)
    one = exchange(
        pack((tangent_queries, queries, *kv), ((0, tokens), (0, half), (0, half)))
    )
    two = exchange(pack(kv, ((half, half), (half, half))))
    state = call(first_kernel, "first", one, one, half, tokens, 0, tokens, None, 0, 512)
    outs = []
    for part in range(2):
        q_rows = tokens // 2
        outs.append(
            exchange(
                call(
                    last_kernel,
                    f"last_{part}",
                    one,
                    two,
                    half,
                    0,
                    part * q_rows,
                    q_rows,
                    state,
                    part * q_rows // 16,
                    512,
                )
            )
        )
    return tuple(unpack(outs))


def solution(mesh):
    split = P(("clip", "ctx"), None)
    return jax.shard_map(
        body, mesh=mesh, in_specs=(split,) * 6, out_specs=(split, split), check_vma=False
    )
```

time: 315 us -> 176 us (0.56)
  matrix products: 99.6 us -> 0 us
  Pallas kernels: 0 us -> 73 us
  waiting for transfers between devices: 105 us -> 55.4 us
  other arithmetic: 33 us -> 0 us
  local copies, waits for them, and re-layouts: 33.9 us -> 1.35 us
  blocking collectives: 0 us -> 22.6 us
  starting transfers between devices: 40.3 us -> 22.4 us
    dot_general x48 -> x0, matrix products: 99.6 us -> none  [the longest x8 23.7 us: tangent_block(): jnp.einsum('qhd,khd->hqk', query_block, tkey_all, preferred_element_type=...]
    pallas_call x0 -> x6, Pallas kernels: none -> 73 us  [the longest x3 53.6 us: call(): pl.pallas_call(functools.partial(kernel, chunk), grid=(steps,), in_specs=...]
    all_to_all x8 -> x3, waiting for transfers between devices: 105 us -> 55.4 us  [exchange(): return lax.all_to_all(array, 'ctx', split_axis=0, concat_axis=0, tiled=True)]
    all_to_all x0 -> x1, blocking collectives: none -> 22.6 us  [exchange(): return lax.all_to_all(array, 'ctx', split_axis=0, concat_axis=0, tiled=True)]
    unnamed x16 -> x4, local copies, waits for them, and re-layouts: 23.3 us -> 1.35 us
    all_to_all x8 -> x3, starting transfers between devices: 40.3 us -> 22.4 us  [exchange(): return lax.all_to_all(array, 'ctx', split_axis=0, concat_axis=0, tiled=True)]
    div x8 -> x0, other arithmetic: 15.8 us -> none  [probs_block(): return raised / jnp.sum(raised, axis=-1, keepdims=True)]
    reduce_sum x8 -> x0, other arithmetic: 12.1 us -> none  [probs_block(): return raised / jnp.sum(raised, axis=-1, keepdims=True)]
  transfers between devices with their start and end apart: 8 -> 3, of which waited for: 8 -> 3; matrix products, arithmetic and copies ran while one was open for 8% -> 0% of each run, Pallas kernels for 0% -> 26%
where the time goes in v1:
time: 176 us; the launch traced here: 175 us
  Pallas kernels  73 us (41%)
  waiting for transfers between devices  55.4 us (31%)
  blocking collectives  22.6 us (13%)
  starting transfers between devices  22.4 us (13%)
    all_to_all x3, waiting for transfers between devices, exchange(): return lax.all_to_all(array, 'ctx', split_axis=0, concat_axis=0, tiled=True)  55.4 us
    pallas_call x3, Pallas kernels, call(): pl.pallas_call(functools.partial(kernel, chunk), grid=(steps,), in_specs=...  53.6 us
    all_to_all x1, blocking collectives, exchange(): return lax.all_to_all(array, 'ctx', split_axis=0, concat_axis=0, tiled=True)  22.6 us
    all_to_all x3, starting transfers between devices, exchange(): return lax.all_to_all(array, 'ctx', split_axis=0, concat_axis=0, tiled=True)  22.4 us
    pallas_call x2, Pallas kernels, pack(): pl.pallas_call(functools.partial(pack_kernel, pairs, heads), grid=(groups...  13.5 us
    pallas_call x1, Pallas kernels, unpack(): pl.pallas_call(functools.partial(unpack_kernel, heads, len(parts)), grid=...  5.83 us
  transfers between devices with their start and end apart: 3, of which 3 were waited for; matrix products, arithmetic and copies ran while one was open for 0% of the time, Pallas kernels for 26%

profile of v1, /device:TPU:0, one launch (start us, length us, event | category | flops | bytes accessed | tf_op | source)
XLA Modules:
  0.0 175.3 jit_solution(1818493699811176060)
XLA Ops:
  0.6 7.3 %pack.2 = bf16[32,256,256]{2,1,0:T(8,128)(2,1)} custom-call(bf16[128,4096]{1,0:T(8,128)(2,1)} %refs_0_.2, bf16[128,4096]{1,0:T(8,128)(2,1)} %refs_1_.2, bf16[128,4096]{1,0:T(8,128)(2,1)} %refs_0_.3, bf16[128,4096]{1,0:T(8,128)(2,1)} %refs_1_.3, bf16[128,4096]{1,0:T(8,128)(2,1)} %refs_2_.3, bf16[128,4096]{1,0:T(8,128)(2,1)} %refs_3_.3), custom_call_target="tpu_custom_call" | custom-call | bytes 8388608 | tf_op jit(solution)/shard_map/pack/pallas_call | solution.py:44
  7.9 9.4 %all-to-all-start = ((bf16[32,256,256]{2,1,0:T(8,128)(2,1)}), bf16[32,256,256]{2,1,0:T(8,128)(2,1)}, u32[]{:S(2)}, u32[]{:S(2)}) async-start(bf16[32,256,256]{2,1,0:T(8,128)(2,1)} %pack.2), calls=%async_computation | async-start | bytes 8388608 | tf_op jit(solution)/shard_map/all_to_all | solution.py:208
  17.4 6.2 %pack.3 = bf16[32,128,256]{2,1,0:T(8,128)(2,1)} custom-call(bf16[128,4096]{1,0:T(8,128)(2,1)} %refs_0_.3, bf16[128,4096]{1,0:T(8,128)(2,1)} %refs_1_.3, bf16[128,4096]{1,0:T(8,128)(2,1)} %refs_2_.3, bf16[128,4096]{1,0:T(8,128)(2,1)} %refs_3_.3), custom_call_target="tpu_custom_call" | custom-call | bytes 4194304 | tf_op jit(solution)/shard_map/pack/pallas_call | solution.py:44
  23.6 48.2 %all-to-all-done.q_ref.kv_ref = bf16[32,256,256]{2,1,0:T(8,128)(2,1)} async-done(((bf16[32,256,256]{2,1,0:T(8,128)(2,1)}), bf16[32,256,256]{2,1,0:T(8,128)(2,1)}, u32[]{:S(2)}, u32[]{:S(2)}) %all-to-all-start) | async-done | bytes 4194336 | tf_op jit(solution)/shard_map/all_to_all | solution.py:208
  71.8 6.4 %all-to-all-start.1 = ((bf16[32,128,256]{2,1,0:T(8,128)(2,1)}), bf16[32,128,256]{2,1,0:T(8,128)(2,1)S(1)}, u32[]{:S(2)}, u32[]{:S(2)}) async-start(bf16[32,128,256]{2,1,0:T(8,128)(2,1)} %pack.3), calls=%async_computation.1 | async-start | bytes 4194304 | tf_op jit(solution)/shard_map/all_to_all | solution.py:208
  78.1 24.2 %first.1 = (f32[4096,128]{1,0:T(8,128)}, f32[4096,128]{1,0:T(8,128)}, f32[4096,256]{1,0:T(8,128)}, f32[4096,256]{1,0:T(8,128)}) custom-call(bf16[32,256,256]{2,1,0:T(8,128)(2,1)} %all-to-all-done.q_ref.kv_ref, bf16[32,256,256]{2,1,0:T(8,128)(2,1)} %all-to-all-done.q_ref.kv_ref), custom_call_target="tpu_custom_call" | custom-call | flops 17179869184 | bytes 8388608 | tf_op jit(solution)/shard_map/first/pallas_call | solution.py:184
  102.4 4.3 %all-to-all-done.1.kv_ref = bf16[32,128,256]{2,1,0:T(8,128)(2,1)S(1)} async-done(((bf16[32,128,256]{2,1,0:T(8,128)(2,1)}), bf16[32,128,256]{2,1,0:T(8,128)(2,1)S(1)}, u32[]{:S(2)}, u32[]{:S(2)}) %all-to-all-start.1) | async-done | bytes 2097184 | tf_op jit(solution)/shard_map/all_to_all | solution.py:208
  106.6 0.0 copy-start.1
  106.6 1.3 copy-done.1
  108.0 14.7 %last_0.1 = bf16[32,64,256]{2,1,0:T(8,128)(2,1)} custom-call(bf16[32,256,256]{2,1,0:T(8,128)(2,1)} %all-to-all-done.q_ref.kv_ref, bf16[32,128,256]{2,1,0:T(8,128)(2,1)} %copy-done.1, f32[4096,128]{1,0:T(8,128)} %get-tuple-element.6.top, f32[4096,128]{1,0:T(8,128)} %get-tuple-element.7.norm, f32[4096,256]{1,0:T(8,128)} %get-tuple-element.8.both, ...), custom_call_target="tpu_custom_call" | custom-call | flops 8589934592 | bytes 4194304 | tf_op jit(solution)/shard_map/last_0/pallas_call | solution.py:184
  122.7 6.6 %all-to-all-start.2 = ((bf16[32,64,256]{2,1,0:T(8,128)(2,1)}), bf16[32,64,256]{2,1,0:T(8,128)(2,1)S(1)}, u32[]{:S(2)}, u32[]{:S(2)}) async-start(bf16[32,64,256]{2,1,0:T(8,128)(2,1)} %last_0.1), calls=%async_computation.2 | async-start | bytes 2097152 | tf_op jit(solution)/shard_map/all_to_all | solution.py:208
  129.3 14.7 %last_1.1 = bf16[32,64,256]{2,1,0:T(8,128)(2,1)} custom-call(bf16[32,256,256]{2,1,0:T(8,128)(2,1)} %all-to-all-done.q_ref.kv_ref, bf16[32,128,256]{2,1,0:T(8,128)(2,1)} %copy-done.1, f32[4096,128]{1,0:T(8,128)} %get-tuple-element.6.top, f32[4096,128]{1,0:T(8,128)} %get-tuple-element.7.norm, f32[4096,256]{1,0:T(8,128)} %get-tuple-element.8.both, ...), custom_call_target="tpu_custom_call" | custom-call | flops 8589934592 | bytes 4194304 | tf_op jit(solution)/shard_map/last_1/pallas_call | solution.py:184
  144.0 3.0 %all-to-all-done.2.refs_0_ = bf16[32,64,256]{2,1,0:T(8,128)(2,1)S(1)} async-done(((bf16[32,64,256]{2,1,0:T(8,128)(2,1)}), bf16[32,64,256]{2,1,0:T(8,128)(2,1)S(1)}, u32[]{:S(2)}, u32[]{:S(2)}) %all-to-all-start.2) | async-done | bytes 1048608 | tf_op jit(solution)/shard_map/all_to_all | solution.py:208
  146.9 0.0 copy-start
  146.9 22.6 %all_to_all.20.refs_1_ = bf16[32,64,256]{2,1,0:T(8,128)(2,1)} all-to-all(bf16[32,64,256]{2,1,0:T(8,128)(2,1)} %last_1.1), channel_id=1, replica_groups=mesh['clip'=4,'ctx'=32] {'ctx'}, dimensions={0} | all-to-all | bytes 2097152 | tf_op jit(solution)/shard_map/all_to_all | solution.py:208
  169.5 0.0 copy-done
  169.5 5.8 %unpack.1 = (bf16[128,4096]{1,0:T(8,128)(2,1)}, bf16[128,4096]{1,0:T(8,128)(2,1)}) custom-call(bf16[32,64,256]{2,1,0:T(8,128)(2,1)} %copy-done, bf16[32,64,256]{2,1,0:T(8,128)(2,1)} %all_to_all.20.refs_1_), custom_call_target="tpu_custom_call" | custom-call | bytes 4194304 | tf_op jit(solution)/shard_map/unpack/pallas_call | solution.py:73
Async XLA Ops:
  7.9 63.8 %all-to-all-start = ((bf16[32,256,256]{2,1,0:T(8,128)(2,1)}), bf16[32,256,256]{2,1,0:T(8,128)(2,1)}, u32[]{:S(2)}, u32[]{:S(2)}) async-start(bf16[32,256,256]{2,1,0:T(8,128)(2,1)} %pack.2), calls=%async_computation | async-start | bytes 8388608 | tf_op jit(solution)/shard_map/all_to_all | solution.py:208
  71.8 34.9 %all-to-all-start.1 = ((bf16[32,128,256]{2,1,0:T(8,128)(2,1)}), bf16[32,128,256]{2,1,0:T(8,128)(2,1)S(1)}, u32[]{:S(2)}, u32[]{:S(2)}) async-start(bf16[32,128,256]{2,1,0:T(8,128)(2,1)} %pack.3), calls=%async_computation.1 | async-start | bytes 4194304 | tf_op jit(solution)/shard_map/all_to_all | solution.py:208
  106.6 1.3 copy-start.1
  122.7 24.3 %all-to-all-start.2 = ((bf16[32,64,256]{2,1,0:T(8,128)(2,1)}), bf16[32,64,256]{2,1,0:T(8,128)(2,1)S(1)}, u32[]{:S(2)}, u32[]{:S(2)}) async-start(bf16[32,64,256]{2,1,0:T(8,128)(2,1)} %last_0.1), calls=%async_computation.2 | async-start | bytes 2097152 | tf_op jit(solution)/shard_map/all_to_all | solution.py:208
  146.9 22.6 %copy-start = (bf16[32,64,256]{2,1,0:T(8,128)(2,1)}, bf16[32,64,256]{2,1,0:T(8,128)(2,1)S(1)}, u32[]{:S(2)}) copy-start(bf16[32,64,256]{2,1,0:T(8,128)(2,1)S(1)} %all-to-all-done.2.refs_0_) | copy-start | bytes 3145732

commit v2 on v1

v2 whole, which is shorter than its diff:
```python
import functools

import jax
import jax.numpy as jnp
from jax import lax
from jax.experimental import pallas as pl
from jax.experimental.pallas import tpu as pltpu
from jax.sharding import PartitionSpec as P

HD = 128
PAIR = 2 * HD
SCALE = HD**-0.5
TO_LOG2 = 1.4426950408889634 * SCALE
CONTRACT_LAST = (((1,), (1,)), ((), ()))
BF16 = jnp.bfloat16
F32 = jnp.float32
VMEM_BYTES = 62 * 2**20
WIDTHS = (HD, HD, PAIR, PAIR)

FIRST_ROWS = 64
OUT_ROWS = (128,)
LATER_NS = 0
SIDES = 2
SIDE_ROWS = 16
CHUNK = 512
VALUE_CHUNK = 512


def dot_last(a, b):
    return lax.dot_general(a, b, CONTRACT_LAST, preferred_element_type=F32)


def dot(a, b):
    return jnp.dot(a, b, preferred_element_type=F32)


def pack_kernel(pairs, per, late, *refs):
    count = 2 * len(pairs)
    if late:
        flag, refs = refs[0], refs[1:]

        @pl.when(flag[0] == 1)
        def _():
            pl.delay(late)

    ins, (out, held, arrived, left) = refs[:count], refs[count:]
    steps = held.shape[0] // per
    for g in range(steps):
        row = 0
        for which, (start, rows) in enumerate(pairs):
            for side in range(2):
                for h in range(g * per, (g + 1) * per):
                    pltpu.make_async_copy(
                        ins[2 * which + side].at[pl.ds(start, rows), pl.ds(h * HD, HD)],
                        held.at[h, pl.ds(row, rows), pl.ds(side * HD, HD)],
                        arrived.at[g],
                    ).start()
            row += rows
    for g in range(steps):
        group = pl.ds(g * per, per)
        pltpu.make_async_copy(out.at[group], held.at[group], arrived.at[g]).wait()
        pltpu.make_async_copy(held.at[group], out.at[group], left.at[g]).start()
    for g in range(steps):
        group = pl.ds(g * per, per)
        pltpu.make_async_copy(held.at[group], out.at[group], left.at[g]).wait()


def pack(arrays, pairs, later=None, per=8):
    groups = arrays[0].shape[1] // HD
    shape = (groups, sum(rows for _, rows in pairs), PAIR)
    anywhere = pl.BlockSpec(memory_space=pl.ANY)
    late = 0 if later is None else LATER_NS
    flags = [later] if late else []
    return pl.pallas_call(
        functools.partial(pack_kernel, pairs, per, late),
        in_specs=[pl.BlockSpec(memory_space=pltpu.SMEM)] * len(flags) + [anywhere] * len(arrays),
        out_specs=anywhere,
        out_shape=jax.ShapeDtypeStruct(shape, BF16),
        scratch_shapes=[
            pltpu.VMEM(shape, BF16),
            pltpu.SemaphoreType.DMA((groups // per,)),
            pltpu.SemaphoreType.DMA((groups // per,)),
        ],
        cost_estimate=pl.CostEstimate(
            flops=0, bytes_accessed=4 * shape[0] * shape[1] * PAIR, transcendentals=0
        ),
        name="pack",
    )(*flags, *arrays)


def unpack_kernel(per, count, *refs):
    parts, outs, held, arrived, left = (
        refs[:count],
        refs[count : count + 2],
        refs[count + 2 : 2 * count + 2],
        refs[-2],
        refs[-1],
    )
    steps = parts[0].shape[0] // per
    for g in range(steps):
        group = pl.ds(g * per, per)
        for p in range(count):
            pltpu.make_async_copy(
                parts[p].at[group], held[p].at[group], arrived.at[p, g]
            ).start()
    for g in range(steps):
        row = 0
        for p in range(count):
            group = pl.ds(g * per, per)
            rows = held[p].shape[1]
            pltpu.make_async_copy(parts[p].at[group], held[p].at[group], arrived.at[p, g]).wait()
            for h in range(g * per, (g + 1) * per):
                for side in range(2):
                    pltpu.make_async_copy(
                        held[p].at[h, :, pl.ds(side * HD, HD)],
                        outs[side].at[pl.ds(row, rows), pl.ds(h * HD, HD)],
                        left.at[p, g],
                    ).start()
            row += rows
    for g in range(steps):
        for p in range(count):
            group = pl.ds(g * per, per)
            pltpu.make_async_copy(held[p].at[group], parts[p].at[group], left.at[p, g]).wait()


def unpack(parts, per=8):
    groups = parts[0].shape[0]
    tokens = sum(part.shape[1] for part in parts)
    out = jax.ShapeDtypeStruct((tokens, groups * HD), BF16)
    anywhere = pl.BlockSpec(memory_space=pl.ANY)
    return pl.pallas_call(
        functools.partial(unpack_kernel, per, len(parts)),
        in_specs=[anywhere] * len(parts),
        out_specs=[anywhere] * 2,
        out_shape=[out, out],
        scratch_shapes=[pltpu.VMEM(part.shape, BF16) for part in parts]
        + [pltpu.SemaphoreType.DMA((len(parts), groups // per))] * 2,
        cost_estimate=pl.CostEstimate(
            flops=0, bytes_accessed=8 * tokens * groups * HD, transcendentals=0
        ),
        name="unpack",
    )(*parts)


def prepare(kv_ref, twice, ones, keys, vals):
    @pl.when(pl.program_id(0) == 0)
    def _():
        total = keys.shape[0]
        rows = kv_ref.shape[1] // 2
        both = kv_ref[:, :rows, :].reshape(total, PAIR)
        keys[...] = both
        twice[:, :HD] = both[:, :HD]
        twice[:, HD:] = both[:, :HD]
        both = kv_ref[:, rows:, :].reshape(total, PAIR)
        vals[...] = both
        ones[:, :HD] = both[:, :HD]
        ones[:, HD:] = jnp.ones((total, HD), BF16)


class Side:
    def __init__(self, tqq, before, store, held, keyed, chunk):
        scaled = tqq[:, HD:].astype(F32) * TO_LOG2
        high = scaled.astype(BF16)
        low = (scaled - high.astype(F32)).astype(BF16)
        self.tqq, self.query = tqq, jnp.concatenate([high, low], axis=1)
        self.before, self.store, self.chunk, self.block = before, store, chunk, tqq.shape[0]
        self.scores, self.probs, self.weights = held
        self.twice, self.ones, self.keys, self.vals = keyed
        if before is None:
            self.top = jnp.full((self.block, HD), -jnp.inf, F32)
        else:
            self.top = before[0][...]
        self.both = self.tangent = None

    def score(self, start):
        part = dot_last(self.query, self.twice[start : start + self.chunk, :])
        self.scores[:, start : start + self.chunk] = part
        for c in range(0, self.chunk, HD):
            self.top = jnp.maximum(self.top, part[:, c : c + HD])

    def peak(self):
        self.top = jnp.broadcast_to(jnp.max(self.top, axis=1, keepdims=True), (self.block, HD))
        if self.before is None:
            self.norm = jnp.zeros((self.block, HD), F32)
        else:
            self.decay = jnp.exp2(self.before[0][...] - self.top)
            self.norm = self.before[1][...] * self.decay

    def soften(self, start):
        rows = slice(start, start + self.chunk)
        raised = jnp.exp2(self.scores[:, rows] - self.top[:, :1])
        for c in range(0, self.chunk, HD):
            self.norm = self.norm + raised[:, c : c + HD]
        self.probs[:, rows] = raised.astype(BF16)
        self.weights[:, rows] = (raised * dot_last(self.tqq, self.keys[rows, :])).astype(BF16)

    def gather(self, start, size):
        rows = slice(start, start + size)
        both = dot(self.probs[:, rows], self.vals[rows, :])
        tangent = dot(self.weights[:, rows], self.ones[rows, :])
        self.both = both if self.both is None else self.both + both
        self.tangent = tangent if self.tangent is None else self.tangent + tangent

    def finish(self):
        if self.before is not None:
            wide = jnp.concatenate([self.decay, self.decay], axis=1)
            self.both = self.both + self.before[2][...] * wide
            self.tangent = self.tangent + self.before[3][...] * wide
        self.store(self.top, self.norm, self.both, self.tangent)


def attend(sides, total, chunk, value_chunk):
    for start in range(0, total, chunk):
        sides[0].score(start)
    previous = None
    for n, side in enumerate(sides):
        side.peak()
        done = 0
        for start in range(0, total, chunk):
            side.soften(start)
            if n + 1 < len(sides):
                sides[n + 1].score(start)
            while previous is not None and done + value_chunk <= start + chunk:
                previous.gather(done, value_chunk)
                done += value_chunk
        if previous is not None:
            if done < total:
                previous.gather(done, total - done)
            previous.finish()
        previous = side
    previous.gather(0, total)
    previous.finish()


def attention_kernel(count, resumes, ends, q_ref, kv_ref, *refs):
    refs = list(refs)
    take = lambda n: [refs.pop(0) for _ in range(n)]
    state = take(4) if resumes else None
    outs = take(1) if ends else take(4)
    twice, ones, keys, vals = take(4)
    prepare(kv_ref, twice, ones, keys, vals)
    groups, rows = q_ref.shape[0], q_ref.shape[1] // count
    block, total = groups * rows, keys.shape[0]
    sides = []
    for n in range(count):
        mine, tokens = slice(n * block, (n + 1) * block), slice(n * rows, (n + 1) * rows)

        def store(top, norm, both, tangent, mine=mine, tokens=tokens):
            if not ends:
                for ref, value in zip(outs, (top, norm, both, tangent)):
                    ref[mine, :] = value
                return
            share = 1.0 / jnp.sum(norm, axis=1, keepdims=True)
            primal = both[:, :HD] * share
            scaled = tangent * (share * SCALE)
            moved = scaled[:, :HD] + both[:, HD:] * share - scaled[:, HD:] * primal
            outs[0][:, tokens, :HD] = primal.astype(BF16).reshape(groups, rows, HD)
            outs[0][:, tokens, HD:] = moved.astype(BF16).reshape(groups, rows, HD)

        sides.append(
            Side(
                q_ref[:, tokens, :].reshape(block, PAIR),
                [ref.at[mine, :] for ref in state] if resumes else None,
                store,
                take(3),
                (twice, ones, keys, vals),
                CHUNK,
            )
        )
    attend(sides, total, CHUNK, VALUE_CHUNK)


def attention(name, queries, q_at, q_rows, kv, kv_at, kv_rows, state=None, state_at=0, ends=False):
    groups = queries.shape[0]
    rows = SIDES * SIDE_ROWS
    block, total, steps = groups * rows, groups * kv_rows, q_rows // rows
    if ends:
        out_specs = pl.BlockSpec((groups, rows, PAIR), lambda i: (0, i, 0))
        out_shape = jax.ShapeDtypeStruct((groups, q_rows, PAIR), BF16)
    else:
        out_specs = [pl.BlockSpec((block, width), lambda i: (i, 0)) for width in WIDTHS]
        out_shape = [jax.ShapeDtypeStruct((steps * block, width), F32) for width in WIDTHS]
    state_specs = [
        pl.BlockSpec((block, width), lambda i: (i + state_at // rows, 0)) for width in WIDTHS
    ]
    side = groups * SIDE_ROWS
    return pl.pallas_call(
        functools.partial(attention_kernel, SIDES, state is not None, ends),
        grid=(steps,),
        in_specs=[
            pl.BlockSpec((groups, rows, PAIR), lambda i: (0, i + q_at // rows, 0)),
            pl.BlockSpec((groups, 2 * kv_rows, PAIR), lambda i: (0, kv_at // (2 * kv_rows), 0)),
            *(state_specs if state is not None else ()),
        ],
        out_specs=out_specs,
        out_shape=out_shape,
        scratch_shapes=[pltpu.VMEM((total, PAIR), BF16)] * 4
        + [
            pltpu.VMEM((side, total), F32),
            pltpu.VMEM((side, total), BF16),
            pltpu.VMEM((side, total), BF16),
        ]
        * SIDES,
        compiler_params=pltpu.CompilerParams(vmem_limit_bytes=VMEM_BYTES),
        cost_estimate=pl.CostEstimate(
            flops=16 * steps * block * total * HD,
            bytes_accessed=8 * steps * block * PAIR,
            transcendentals=steps * block * total,
        ),
        name=name,
    )(queries, kv, *(state or ()))


def exchange(array):
    return lax.all_to_all(array, "ctx", split_axis=0, concat_axis=0, tiled=True)


def body(queries, key_rows, values, tangent_queries, tangent_keys, tangent_values):
    tokens = queries.shape[0]
    early, rest = FIRST_ROWS, tokens - FIRST_ROWS
    kv = (key_rows, tangent_keys, values, tangent_values)
    later = (lax.axis_index("clip") % 2).astype(jnp.int32).reshape(1)
    one = exchange(
        pack(
            (*kv, tangent_queries, queries), ((0, early), (0, early), (0, tokens)), later
        )
    )
    two = exchange(pack(kv, ((early, rest), (early, rest))))
    q_at = 2 * early
    state = attention("first", one, q_at, tokens, one, 0, early)
    outs, at = [], 0
    for n, rows in enumerate(OUT_ROWS):
        outs.append(
            exchange(
                attention(f"last_{n}", one, q_at + at, rows, two, 0, rest, state, at, True)
            )
        )
        at += rows
    return tuple(unpack(outs))


def solution(mesh):
    split = P(("clip", "ctx"), None)
    return jax.shard_map(
        body, mesh=mesh, in_specs=(split,) * 6, out_specs=(split, split), check_vma=False
    )
```

time: 176 us -> 168 us (0.955)
  Pallas kernels: 73 us -> 58 us
  blocking collectives: 22.6 us -> 35.6 us
  starting transfers between devices: 22.4 us -> 15.9 us
    pallas_call x6 -> x5, Pallas kernels: 73 us -> 58 us  [the longest x2 49.3 us: attention(): pl.pallas_call(functools.partial(attention_kernel, SIDES, state is not No...]
    all_to_all x1, blocking collectives: 22.6 us -> 35.6 us  [exchange(): return lax.all_to_all(array, 'ctx', split_axis=0, concat_axis=0, tiled=True)]
    all_to_all x3 -> x2, starting transfers between devices: 22.4 us -> 15.9 us  [exchange(): return lax.all_to_all(array, 'ctx', split_axis=0, concat_axis=0, tiled=True)]
    all_to_all x3 -> x2, waiting for transfers between devices: 55.4 us -> 56.9 us  [exchange(): return lax.all_to_all(array, 'ctx', split_axis=0, concat_axis=0, tiled=True)]
  transfers between devices with their start and end apart: 3 -> 2, of which waited for: 3 -> 2; matrix products, arithmetic and copies ran while one was open for 0% -> 0% of each run, Pallas kernels for 26% -> 16%
where the time goes in v2:
time: 168 us; the launch traced here: 167 us
  Pallas kernels  58 us (35%)
  waiting for transfers between devices  56.9 us (34%)
  blocking collectives  35.6 us (21%)
  starting transfers between devices  15.9 us (9%)
    all_to_all x2, waiting for transfers between devices, exchange(): return lax.all_to_all(array, 'ctx', split_axis=0, concat_axis=0, tiled=True)  56.9 us
    pallas_call x2, Pallas kernels, attention(): pl.pallas_call(functools.partial(attention_kernel, SIDES, state is not No...  49.3 us
    all_to_all x1, blocking collectives, exchange(): return lax.all_to_all(array, 'ctx', split_axis=0, concat_axis=0, tiled=True)  35.6 us
    all_to_all x2, starting transfers between devices, exchange(): return lax.all_to_all(array, 'ctx', split_axis=0, concat_axis=0, tiled=True)  15.9 us
    pallas_call x2, Pallas kernels, pack(): pl.pallas_call(functools.partial(pack_kernel, pairs, per, late), in_specs...  6.36 us
  transfers between devices with their start and end apart: 2, of which 2 were waited for; matrix products, arithmetic and copies ran while one was open for 0% of the time, Pallas kernels for 16%

profile of v2, /device:TPU:0, one launch (start us, length us, event | category | flops | bytes accessed | tf_op | source)
XLA Modules:
  0.0 167.1 jit_solution(11353669850898875211)
XLA Ops:
  0.6 3.9 %pack.2 = bf16[32,256,256]{2,1,0:T(8,128)(2,1)} custom-call(bf16[128,4096]{1,0:T(8,128)(2,1)} %refs_0_.3, bf16[128,4096]{1,0:T(8,128)(2,1)} %refs_1_.3, bf16[128,4096]{1,0:T(8,128)(2,1)} %refs_2_.3, bf16[128,4096]{1,0:T(8,128)(2,1)} %refs_3_.3, bf16[128,4096]{1,0:T(8,128)(2,1)} %refs_4_.1, bf16[128,4096]{1,0:T(8,128)(2,1)} %refs_5_.1), custom_call_target="tpu_custom_call" | custom-call | bytes 8388608 | tf_op jit(solution)/shard_map/pack/pallas_call | solution.py:74
  4.5 9.4 %all-to-all-start = ((bf16[32,256,256]{2,1,0:T(8,128)(2,1)}), bf16[32,256,256]{2,1,0:T(8,128)(2,1)}, u32[]{:S(2)}, u32[]{:S(2)}) async-start(bf16[32,256,256]{2,1,0:T(8,128)(2,1)} %pack.2), calls=%async_computation | async-start | bytes 8388608 | tf_op jit(solution)/shard_map/all_to_all | solution.py:315
  14.0 2.5 %pack.3 = bf16[32,128,256]{2,1,0:T(8,128)(2,1)} custom-call(bf16[128,4096]{1,0:T(8,128)(2,1)} %refs_0_.3, bf16[128,4096]{1,0:T(8,128)(2,1)} %refs_1_.3, bf16[128,4096]{1,0:T(8,128)(2,1)} %refs_2_.3, bf16[128,4096]{1,0:T(8,128)(2,1)} %refs_3_.3), custom_call_target="tpu_custom_call" | custom-call | bytes 4194304 | tf_op jit(solution)/shard_map/pack/pallas_call | solution.py:74
  16.4 51.9 %all-to-all-done.q_ref.kv_ref = bf16[32,256,256]{2,1,0:T(8,128)(2,1)} async-done(((bf16[32,256,256]{2,1,0:T(8,128)(2,1)}), bf16[32,256,256]{2,1,0:T(8,128)(2,1)}, u32[]{:S(2)}, u32[]{:S(2)}) %all-to-all-start) | async-done | bytes 4194336 | tf_op jit(solution)/shard_map/all_to_all | solution.py:315
  68.4 6.5 %all-to-all-start.1 = ((bf16[32,128,256]{2,1,0:T(8,128)(2,1)}), bf16[32,128,256]{2,1,0:T(8,128)(2,1)}, u32[]{:S(2)}, u32[]{:S(2)}) async-start(bf16[32,128,256]{2,1,0:T(8,128)(2,1)} %pack.3), calls=%async_computation.1 | async-start | bytes 4194304 | tf_op jit(solution)/shard_map/all_to_all | solution.py:315
  74.9 23.5 %first.1 = (f32[4096,128]{1,0:T(8,128)}, f32[4096,128]{1,0:T(8,128)}, f32[4096,256]{1,0:T(8,128)}, f32[4096,256]{1,0:T(8,128)}) custom-call(bf16[32,256,256]{2,1,0:T(8,128)(2,1)} %all-to-all-done.q_ref.kv_ref, bf16[32,256,256]{2,1,0:T(8,128)(2,1)} %all-to-all-done.q_ref.kv_ref), custom_call_target="tpu_custom_call" | custom-call | flops 17179869184 | bytes 8388608 | tf_op jit(solution)/shard_map/first/pallas_call | solution.py:287
  98.4 4.9 %all-to-all-done.1.kv_ref = bf16[32,128,256]{2,1,0:T(8,128)(2,1)} async-done(((bf16[32,128,256]{2,1,0:T(8,128)(2,1)}), bf16[32,128,256]{2,1,0:T(8,128)(2,1)}, u32[]{:S(2)}, u32[]{:S(2)}) %all-to-all-start.1) | async-done | bytes 2097184 | tf_op jit(solution)/shard_map/all_to_all | solution.py:315
  103.3 25.7 %last_0.1 = bf16[32,128,256]{2,1,0:T(8,128)(2,1)} custom-call(bf16[32,256,256]{2,1,0:T(8,128)(2,1)} %all-to-all-done.q_ref.kv_ref, bf16[32,128,256]{2,1,0:T(8,128)(2,1)} %all-to-all-done.1.kv_ref, f32[4096,128]{1,0:T(8,128)} %get-tuple-element.6.refs_0_, f32[4096,128]{1,0:T(8,128)} %get-tuple-element.7.refs_1_, f32[4096,256]{1,0:T(8,128)} %get-tuple-element.8.refs_2_, ...), custom_call_target="tpu_custom_call" | custom-call | flops 17179869184 | bytes 8388608 | tf_op jit(solution)/shard_map/last_0/pallas_call | solution.py:287
  129.1 35.6 %all_to_all.15.refs_0_ = bf16[32,128,256]{2,1,0:T(8,128)(2,1)} all-to-all(bf16[32,128,256]{2,1,0:T(8,128)(2,1)} %last_0.1), channel_id=1, replica_groups=mesh['clip'=4,'ctx'=32] {'ctx'}, dimensions={0} | all-to-all | bytes 4194304 | tf_op jit(solution)/shard_map/all_to_all | solution.py:315
  164.7 2.4 %unpack.1 = (bf16[128,4096]{1,0:T(8,128)(2,1)}, bf16[128,4096]{1,0:T(8,128)(2,1)}) custom-call(bf16[32,128,256]{2,1,0:T(8,128)(2,1)} %all_to_all.15.refs_0_), custom_call_target="tpu_custom_call" | custom-call | bytes 4194304 | tf_op jit(solution)/shard_map/unpack/pallas_call | solution.py:131
Async XLA Ops:
  4.5 63.8 %all-to-all-start = ((bf16[32,256,256]{2,1,0:T(8,128)(2,1)}), bf16[32,256,256]{2,1,0:T(8,128)(2,1)}, u32[]{:S(2)}, u32[]{:S(2)}) async-start(bf16[32,256,256]{2,1,0:T(8,128)(2,1)} %pack.2), calls=%async_computation | async-start | bytes 8388608 | tf_op jit(solution)/shard_map/all_to_all | solution.py:315
  68.4 35.0 %all-to-all-start.1 = ((bf16[32,128,256]{2,1,0:T(8,128)(2,1)}), bf16[32,128,256]{2,1,0:T(8,128)(2,1)}, u32[]{:S(2)}, u32[]{:S(2)}) async-start(bf16[32,128,256]{2,1,0:T(8,128)(2,1)} %pack.3), calls=%async_computation.1 | async-start | bytes 4194304 | tf_op jit(solution)/shard_map/all_to_all | solution.py:315

commit v3 on v2

--- a/solution.py
+++ b/solution.py
@@ -18,8 +18,9 @@
 WIDTHS = (HD, HD, PAIR, PAIR)
 
 FIRST_ROWS = 64
+AHEAD_ROWS = 48
 OUT_ROWS = (128,)
-LATER_NS = 0
+LATER_NS = 25000
 SIDES = 2
 SIDE_ROWS = 16
 CHUNK = 512
@@ -37,12 +38,7 @@
 def pack_kernel(pairs, per, late, *refs):
     count = 2 * len(pairs)
     if late:
-        flag, refs = refs[0], refs[1:]
-
-        @pl.when(flag[0] == 1)
-        def _():
-            pl.delay(late)
-
+        pl.delay(late)
     ins, (out, held, arrived, left) = refs[:count], refs[count:]
     steps = held.shape[0] // per
     for g in range(steps):
@@ -65,15 +61,13 @@
         pltpu.make_async_copy(held.at[group], out.at[group], left.at[g]).wait()
 
 
-def pack(arrays, pairs, later=None, per=8):
+def pack(arrays, pairs, late=0, per=8):
     groups = arrays[0].shape[1] // HD
     shape = (groups, sum(rows for _, rows in pairs), PAIR)
     anywhere = pl.BlockSpec(memory_space=pl.ANY)
-    late = 0 if later is None else LATER_NS
-    flags = [later] if late else []
     return pl.pallas_call(
         functools.partial(pack_kernel, pairs, per, late),
-        in_specs=[pl.BlockSpec(memory_space=pltpu.SMEM)] * len(flags) + [anywhere] * len(arrays),
+        in_specs=[anywhere] * len(arrays),
         out_specs=anywhere,
         out_shape=jax.ShapeDtypeStruct(shape, BF16),
         scratch_shapes=[
@@ -85,7 +79,7 @@
             flops=0, bytes_accessed=4 * shape[0] * shape[1] * PAIR, transcendentals=0
         ),
         name="pack",
-    )(*flags, *arrays)
+    )(*arrays)
 
 
 def unpack_kernel(per, count, *refs):
@@ -142,15 +136,12 @@
     )(*parts)
 
 
-def prepare(kv_ref, twice, ones, keys, vals):
+def prepare(kv_ref, ones, keys, vals):
     @pl.when(pl.program_id(0) == 0)
     def _():
         total = keys.shape[0]
         rows = kv_ref.shape[1] // 2
-        both = kv_ref[:, :rows, :].reshape(total, PAIR)
-        keys[...] = both
-        twice[:, :HD] = both[:, :HD]
-        twice[:, HD:] = both[:, :HD]
+        keys[...] = kv_ref[:, :rows, :].reshape(total, PAIR)
         both = kv_ref[:, rows:, :].reshape(total, PAIR)
         vals[...] = both
         ones[:, :HD] = both[:, :HD]
@@ -159,13 +150,10 @@
 
 class Side:
     def __init__(self, tqq, before, store, held, keyed, chunk):
-        scaled = tqq[:, HD:].astype(F32) * TO_LOG2
-        high = scaled.astype(BF16)
-        low = (scaled - high.astype(F32)).astype(BF16)
-        self.tqq, self.query = tqq, jnp.concatenate([high, low], axis=1)
+        self.tqq, self.query = tqq, tqq[:, HD:]
         self.before, self.store, self.chunk, self.block = before, store, chunk, tqq.shape[0]
         self.scores, self.probs, self.weights = held
-        self.twice, self.ones, self.keys, self.vals = keyed
+        self.ones, self.keys, self.vals = keyed
         if before is None:
             self.top = jnp.full((self.block, HD), -jnp.inf, F32)
         else:
@@ -173,7 +161,7 @@
         self.both = self.tangent = None
 
     def score(self, start):
-        part = dot_last(self.query, self.twice[start : start + self.chunk, :])
+        part = dot_last(self.query, self.keys[start : start + self.chunk, :HD])
         self.scores[:, start : start + self.chunk] = part
         for c in range(0, self.chunk, HD):
             self.top = jnp.maximum(self.top, part[:, c : c + HD])
@@ -183,12 +171,12 @@
         if self.before is None:
             self.norm = jnp.zeros((self.block, HD), F32)
         else:
-            self.decay = jnp.exp2(self.before[0][...] - self.top)
+            self.decay = jnp.exp2((self.before[0][...] - self.top) * TO_LOG2)
             self.norm = self.before[1][...] * self.decay
 
     def soften(self, start):
         rows = slice(start, start + self.chunk)
-        raised = jnp.exp2(self.scores[:, rows] - self.top[:, :1])
+        raised = jnp.exp2((self.scores[:, rows] - self.top[:, :1]) * TO_LOG2)
         for c in range(0, self.chunk, HD):
             self.norm = self.norm + raised[:, c : c + HD]
         self.probs[:, rows] = raised.astype(BF16)
@@ -237,8 +225,8 @@
     take = lambda n: [refs.pop(0) for _ in range(n)]
     state = take(4) if resumes else None
     outs = take(1) if ends else take(4)
-    twice, ones, keys, vals = take(4)
-    prepare(kv_ref, twice, ones, keys, vals)
+    ones, keys, vals = take(3)
+    prepare(kv_ref, ones, keys, vals)
     groups, rows = q_ref.shape[0], q_ref.shape[1] // count
     block, total = groups * rows, keys.shape[0]
     sides = []
@@ -263,7 +251,7 @@
                 [ref.at[mine, :] for ref in state] if resumes else None,
                 store,
                 take(3),
-                (twice, ones, keys, vals),
+                (ones, keys, vals),
                 CHUNK,
             )
         )
@@ -294,7 +282,7 @@
         ],
         out_specs=out_specs,
         out_shape=out_shape,
-        scratch_shapes=[pltpu.VMEM((total, PAIR), BF16)] * 4
+        scratch_shapes=[pltpu.VMEM((total, PAIR), BF16)] * 3
         + [
             pltpu.VMEM((side, total), F32),
             pltpu.VMEM((side, total), BF16),
@@ -315,19 +303,27 @@
     return lax.all_to_all(array, "ctx", split_axis=0, concat_axis=0, tiled=True)
 
 
-def body(queries, key_rows, values, tangent_queries, tangent_keys, tangent_values):
+def run(ahead, queries, key_rows, values, tangent_queries, tangent_keys, tangent_values):
     tokens = queries.shape[0]
-    early, rest = FIRST_ROWS, tokens - FIRST_ROWS
+    early = AHEAD_ROWS if ahead else FIRST_ROWS
+    rest = tokens - early
     kv = (key_rows, tangent_keys, values, tangent_values)
-    later = (lax.axis_index("clip") % 2).astype(jnp.int32).reshape(1)
     one = exchange(
         pack(
-            (*kv, tangent_queries, queries), ((0, early), (0, early), (0, tokens)), later
+            (*kv, tangent_queries, queries),
+            ((0, early), (0, early), (0, tokens)),
+            0 if ahead else LATER_NS,
         )
     )
-    two = exchange(pack(kv, ((early, rest), (early, rest))))
+    two = pack(kv, ((early, rest), (early, rest)))
     q_at = 2 * early
-    state = attention("first", one, q_at, tokens, one, 0, early)
+    if ahead:
+        state = attention("first", one, q_at, tokens, one, 0, early)
+        two, *state = lax.optimization_barrier((two, *state))
+        two = exchange(two)
+    else:
+        two = exchange(two)
+        state = attention("first", one, q_at, tokens, one, 0, early)
     outs, at = [], 0
     for n, rows in enumerate(OUT_ROWS):
         outs.append(
@@ -339,6 +335,13 @@
     return tuple(unpack(outs))
 
 
+def body(*arrays):
+    ahead = lax.axis_index("clip") % 2 == 1
+    return lax.cond(
+        ahead, functools.partial(run, True), functools.partial(run, False), *arrays
+    )
+
+
 def solution(mesh):
     split = P(("clip", "ctx"), None)
     return jax.shard_map(

time: 168 us -> 160 us (0.952)
  waiting for transfers between devices: 56.9 us -> 31.4 us
  Pallas kernels: 58 us -> 82.1 us
  blocking collectives: 35.6 us -> 27.2 us
    all_to_all x2, waiting for transfers between devices: 56.9 us -> 31.4 us  [exchange(): return lax.all_to_all(array, 'ctx', split_axis=0, concat_axis=0, tiled=True)]
    pallas_call x2, Pallas kernels: 6.36 us -> 31.3 us  [pack(): pl.pallas_call(functools.partial(pack_kernel, pairs, per, late), in_specs...]
    all_to_all x1, blocking collectives: 35.6 us -> 27.2 us  [exchange(): return lax.all_to_all(array, 'ctx', split_axis=0, concat_axis=0, tiled=True)]
  transfers between devices with their start and end apart: 2 -> 2, of which waited for: 2 -> 1; matrix products, arithmetic and copies ran while one was open for 0% -> 0% of each run, Pallas kernels for 16% -> 16%
where the time goes in v3:
time: 160 us; the launch traced here: 159 us
  Pallas kernels  82.1 us (51%)
  waiting for transfers between devices  31.4 us (20%)
  blocking collectives  27.2 us (17%)
  starting transfers between devices  17.3 us (11%)
    pallas_call x2, Pallas kernels, attention(): pl.pallas_call(functools.partial(attention_kernel, SIDES, state is not No...  48.4 us
    all_to_all x2, waiting for transfers between devices, exchange(): return lax.all_to_all(array, 'ctx', split_axis=0, concat_axis=0, tiled=True)  31.4 us
    pallas_call x2, Pallas kernels, pack(): pl.pallas_call(functools.partial(pack_kernel, pairs, per, late), in_specs...  31.3 us
    all_to_all x1, blocking collectives, exchange(): return lax.all_to_all(array, 'ctx', split_axis=0, concat_axis=0, tiled=True)  27.2 us
    all_to_all x2, starting transfers between devices, exchange(): return lax.all_to_all(array, 'ctx', split_axis=0, concat_axis=0, tiled=True)  17.3 us
  transfers between devices with their start and end apart: 2, of which 1 were waited for; matrix products, arithmetic and copies ran while one was open for 0% of the time, Pallas kernels for 16%

profile of v3, /device:TPU:0, one launch (start us, length us, event | category | flops | bytes accessed | tf_op | source)
XLA Modules:
  0.0 159.4 jit_solution(3624200695032843379)
XLA Ops:
  0.6 158.5 %conditional.1 = ((bf16[128,4096]{1,0:T(8,128)(2,1)}, bf16[128,4096]{1,0:T(8,128)(2,1)})) conditional(s32[]{:T(128)} %convert_element_type.3, (bf16[128,4096]{1,0:T(8,128)(2,1)}, bf16[128,4096]{1,0:T(8,128)(2,1)}, bf16[128,4096]{1,0:T(8,128)(2,1)}, bf16[128,4096]{1,0:T(8,128)(2,1)}, bf16[128,4096]{1,0:T(8,128)(2,1)}, ...), branch_computations={%region_0.1_spmd, %region_1.2_spmd} | conditional | flops 34359738368 | bytes 69206168 | solution.py:340
  0.7 29.0 %pack.4 = bf16[32,256,256]{2,1,0:T(8,128)(2,1)} custom-call(bf16[128,4096]{1,0:T(8,128)(2,1)} %get-tuple-element.24.refs_0_, bf16[128,4096]{1,0:T(8,128)(2,1)} %get-tuple-element.25.refs_1_, bf16[128,4096]{1,0:T(8,128)(2,1)} %get-tuple-element.26.refs_2_, bf16[128,4096]{1,0:T(8,128)(2,1)} %get-tuple-element.27.refs_3_, ...), custom_call_target="tpu_custom_call" | custom-call | bytes 8388608 | tf_op jit(solution)/shard_map/cond/branch_0_fun/pack/pallas_call | solution.py:68
  29.6 0.0 copy-start
  29.6 0.0 copy-start.2
  29.6 0.0 copy-start.4
  29.6 9.7 %all-to-all-start = ((bf16[32,256,256]{2,1,0:T(8,128)(2,1)}), bf16[32,256,256]{2,1,0:T(8,128)(2,1)}, u32[]{:S(2)}, u32[]{:S(2)}) async-start(bf16[32,256,256]{2,1,0:T(8,128)(2,1)} %pack.4), calls=%async_computation | async-start | bytes 8388608 | tf_op jit(solution)/shard_map/cond/branch_0_fun/all_to_all | solution.py:303
  39.3 0.0 copy-done
  39.4 0.0 copy-done.2
  39.4 0.0 copy-done.4
  39.4 2.3 %pack.5 = bf16[32,128,256]{2,1,0:T(8,128)(2,1)} custom-call(bf16[128,4096]{1,0:T(8,128)(2,1)S(1)} %copy-done, bf16[128,4096]{1,0:T(8,128)(2,1)S(1)} %copy-done.2, bf16[128,4096]{1,0:T(8,128)(2,1)S(1)} %copy-done.4, bf16[128,4096]{1,0:T(8,128)(2,1)} %get-tuple-element.27.refs_3_), custom_call_target="tpu_custom_call" | custom-call | bytes 4194304 | tf_op jit(solution)/shard_map/cond/branch_0_fun/pack/pallas_call | solution.py:68
  41.7 31.4 %all-to-all-done.q_ref.kv_ref = bf16[32,256,256]{2,1,0:T(8,128)(2,1)} async-done(((bf16[32,256,256]{2,1,0:T(8,128)(2,1)}), bf16[32,256,256]{2,1,0:T(8,128)(2,1)}, u32[]{:S(2)}, u32[]{:S(2)}) %all-to-all-start) | async-done | bytes 4194336 | tf_op jit(solution)/shard_map/cond/branch_0_fun/all_to_all | solution.py:303
  73.1 7.6 %all-to-all-start.1 = ((bf16[32,128,256]{2,1,0:T(8,128)(2,1)}), bf16[32,128,256]{2,1,0:T(8,128)(2,1)}, u32[]{:S(2)}, u32[]{:S(2)}) async-start(bf16[32,128,256]{2,1,0:T(8,128)(2,1)} %pack.5), calls=%async_computation.1 | async-start | bytes 4194304 | tf_op jit(solution)/shard_map/cond/branch_0_fun/all_to_all | solution.py:303
  80.7 23.0 %first.2 = (f32[4096,128]{1,0:T(8,128)}, f32[4096,128]{1,0:T(8,128)}, f32[4096,256]{1,0:T(8,128)}, f32[4096,256]{1,0:T(8,128)}) custom-call(bf16[32,256,256]{2,1,0:T(8,128)(2,1)} %all-to-all-done.q_ref.kv_ref, bf16[32,256,256]{2,1,0:T(8,128)(2,1)} %all-to-all-done.q_ref.kv_ref), custom_call_target="tpu_custom_call" | custom-call | flops 17179869184 | bytes 8388608 | tf_op jit(solution)/shard_map/cond/branch_0_fun/first/pallas_call | solution.py:275
  103.8 0.0 all-to-all-done.1.kv_ref
  103.8 25.4 %last_0.2 = bf16[32,128,256]{2,1,0:T(8,128)(2,1)} custom-call(bf16[32,256,256]{2,1,0:T(8,128)(2,1)} %all-to-all-done.q_ref.kv_ref, bf16[32,128,256]{2,1,0:T(8,128)(2,1)} %all-to-all-done.1.kv_ref, f32[4096,128]{1,0:T(8,128)} %get-tuple-element.30.refs_0_, f32[4096,128]{1,0:T(8,128)} %get-tuple-element.31.refs_1_, f32[4096,256]{1,0:T(8,128)} %get-tuple-element.32.refs_2_, ...), custom_call_target="tpu_custom_call" | custom-call | flops 17179869184 | bytes 8388608 | tf_op jit(solution)/shard_map/cond/branch_0_fun/last_0/pallas_call | solution.py:275
  129.1 27.2 %all_to_all.24.refs_0_ = bf16[32,128,256]{2,1,0:T(8,128)(2,1)} all-to-all(bf16[32,128,256]{2,1,0:T(8,128)(2,1)} %last_0.2), channel_id=1, replica_groups=mesh['clip'=4,'ctx'=32] {'ctx'}, dimensions={0} | all-to-all | bytes 4194304 | tf_op jit(solution)/shard_map/cond/branch_0_fun/all_to_all | solution.py:303
  156.3 2.4 %unpack.2 = (bf16[128,4096]{1,0:T(8,128)(2,1)}, bf16[128,4096]{1,0:T(8,128)(2,1)}) custom-call(bf16[32,128,256]{2,1,0:T(8,128)(2,1)} %all_to_all.24.refs_0_), custom_call_target="tpu_custom_call" | custom-call | bytes 4194304 | tf_op jit(solution)/shard_map/cond/branch_0_fun/unpack/pallas_call | solution.py:125
Async XLA Ops:
  29.6 9.7 %copy-start = (bf16[128,4096]{1,0:T(8,128)(2,1)S(1)}, bf16[128,4096]{1,0:T(8,128)(2,1)}, u32[]{:S(2)}) copy-start(bf16[128,4096]{1,0:T(8,128)(2,1)} %get-tuple-element.24.refs_0_) | copy-start | bytes 3145732 | tf_op jit(solution)/shard_map/cond
  29.6 9.7 %copy-start.2 = (bf16[128,4096]{1,0:T(8,128)(2,1)S(1)}, bf16[128,4096]{1,0:T(8,128)(2,1)}, u32[]{:S(2)}) copy-start(bf16[128,4096]{1,0:T(8,128)(2,1)} %get-tuple-element.25.refs_1_) | copy-start | bytes 3145732 | tf_op jit(solution)/shard_map/cond
  29.6 9.7 %copy-start.4 = (bf16[128,4096]{1,0:T(8,128)(2,1)S(1)}, bf16[128,4096]{1,0:T(8,128)(2,1)}, u32[]{:S(2)}) copy-start(bf16[128,4096]{1,0:T(8,128)(2,1)} %get-tuple-element.26.refs_2_) | copy-start | bytes 3145732 | tf_op jit(solution)/shard_map/cond
  29.6 43.4 %all-to-all-start = ((bf16[32,256,256]{2,1,0:T(8,128)(2,1)}), bf16[32,256,256]{2,1,0:T(8,128)(2,1)}, u32[]{:S(2)}, u32[]{:S(2)}) async-start(bf16[32,256,256]{2,1,0:T(8,128)(2,1)} %pack.4), calls=%async_computation | async-start | bytes 8388608 | tf_op jit(solution)/shard_map/cond/branch_0_fun/all_to_all | solution.py:303
  73.1 30.7 %all-to-all-start.1 = ((bf16[32,128,256]{2,1,0:T(8,128)(2,1)}), bf16[32,128,256]{2,1,0:T(8,128)(2,1)}, u32[]{:S(2)}, u32[]{:S(2)}) async-start(bf16[32,128,256]{2,1,0:T(8,128)(2,1)} %pack.5), calls=%async_computation.1 | async-start | bytes 4194304 | tf_op jit(solution)/shard_map/cond/branch_0_fun/all_to_all | solution.py:303

commit v4 on v3

--- a/solution.py
+++ b/solution.py
@@ -20,7 +20,7 @@
 FIRST_ROWS = 64
 AHEAD_ROWS = 48
 OUT_ROWS = (128,)
-LATER_NS = 25000
+LATER_NS = 24500
 SIDES = 2
 SIDE_ROWS = 16
 CHUNK = 512

time: 160 us -> 160 us (level)
  no operation moved by 1% of the time
where the time goes in v4:
time: 160 us
  Pallas kernels  81.6 us (51%)
  waiting for transfers between devices  30.9 us (19%)
  blocking collectives  27.2 us (17%)
  starting transfers between devices  18.5 us (12%)
    pallas_call x2, Pallas kernels, attention(): pl.pallas_call(functools.partial(attention_kernel, SIDES, state is not No...  48.4 us
    all_to_all x2, waiting for transfers between devices, exchange(): return lax.all_to_all(array, 'ctx', split_axis=0, concat_axis=0, tiled=True)  30.9 us
    pallas_call x2, Pallas kernels, pack(): pl.pallas_call(functools.partial(pack_kernel, pairs, per, late), in_specs...  30.8 us
    all_to_all x1, blocking collectives, exchange(): return lax.all_to_all(array, 'ctx', split_axis=0, concat_axis=0, tiled=True)  27.2 us
    all_to_all x2, starting transfers between devices, exchange(): return lax.all_to_all(array, 'ctx', split_axis=0, concat_axis=0, tiled=True)  18.5 us
  transfers between devices with their start and end apart: 2, of which 1 were waited for; matrix products, arithmetic and copies ran while one was open for 0% of the time, Pallas kernels for 16%

profile of v4, /device:TPU:0, one launch (start us, length us, event | category | flops | bytes accessed | tf_op | source)
XLA Modules:
  0.0 159.6 jit_solution(8642233185731513206)
XLA Ops:
  0.6 158.7 %conditional.1 = ((bf16[128,4096]{1,0:T(8,128)(2,1)}, bf16[128,4096]{1,0:T(8,128)(2,1)})) conditional(s32[]{:T(128)} %convert_element_type.3, (bf16[128,4096]{1,0:T(8,128)(2,1)}, bf16[128,4096]{1,0:T(8,128)(2,1)}, bf16[128,4096]{1,0:T(8,128)(2,1)}, bf16[128,4096]{1,0:T(8,128)(2,1)}, bf16[128,4096]{1,0:T(8,128)(2,1)}, ...), branch_computations={%region_0.1_spmd, %region_1.2_spmd} | conditional | flops 34359738368 | bytes 69206168 | solution.py:340
  0.7 28.5 %pack.4 = bf16[32,256,256]{2,1,0:T(8,128)(2,1)} custom-call(bf16[128,4096]{1,0:T(8,128)(2,1)} %get-tuple-element.24.refs_0_, bf16[128,4096]{1,0:T(8,128)(2,1)} %get-tuple-element.25.refs_1_, bf16[128,4096]{1,0:T(8,128)(2,1)} %get-tuple-element.26.refs_2_, bf16[128,4096]{1,0:T(8,128)(2,1)} %get-tuple-element.27.refs_3_, ...), custom_call_target="tpu_custom_call" | custom-call | bytes 8388608 | tf_op jit(solution)/shard_map/cond/branch_0_fun/pack/pallas_call | solution.py:68
  29.1 0.0 copy-start
  29.1 0.0 copy-start.2
  29.1 0.0 copy-start.4
  29.1 9.7 %all-to-all-start = ((bf16[32,256,256]{2,1,0:T(8,128)(2,1)}), bf16[32,256,256]{2,1,0:T(8,128)(2,1)}, u32[]{:S(2)}, u32[]{:S(2)}) async-start(bf16[32,256,256]{2,1,0:T(8,128)(2,1)} %pack.4), calls=%async_computation | async-start | bytes 8388608 | tf_op jit(solution)/shard_map/cond/branch_0_fun/all_to_all | solution.py:303
  38.8 0.0 copy-done
  38.9 0.0 copy-done.2
  38.9 0.0 copy-done.4
  38.9 2.3 %pack.5 = bf16[32,128,256]{2,1,0:T(8,128)(2,1)} custom-call(bf16[128,4096]{1,0:T(8,128)(2,1)S(1)} %copy-done, bf16[128,4096]{1,0:T(8,128)(2,1)S(1)} %copy-done.2, bf16[128,4096]{1,0:T(8,128)(2,1)S(1)} %copy-done.4, bf16[128,4096]{1,0:T(8,128)(2,1)} %get-tuple-element.27.refs_3_), custom_call_target="tpu_custom_call" | custom-call | bytes 4194304 | tf_op jit(solution)/shard_map/cond/branch_0_fun/pack/pallas_call | solution.py:68
  41.2 30.9 %all-to-all-done.q_ref.kv_ref = bf16[32,256,256]{2,1,0:T(8,128)(2,1)} async-done(((bf16[32,256,256]{2,1,0:T(8,128)(2,1)}), bf16[32,256,256]{2,1,0:T(8,128)(2,1)}, u32[]{:S(2)}, u32[]{:S(2)}) %all-to-all-start) | async-done | bytes 4194336 | tf_op jit(solution)/shard_map/cond/branch_0_fun/all_to_all | solution.py:303
  72.1 8.8 %all-to-all-start.1 = ((bf16[32,128,256]{2,1,0:T(8,128)(2,1)}), bf16[32,128,256]{2,1,0:T(8,128)(2,1)}, u32[]{:S(2)}, u32[]{:S(2)}) async-start(bf16[32,128,256]{2,1,0:T(8,128)(2,1)} %pack.5), calls=%async_computation.1 | async-start | bytes 4194304 | tf_op jit(solution)/shard_map/cond/branch_0_fun/all_to_all | solution.py:303
  80.9 23.0 %first.2 = (f32[4096,128]{1,0:T(8,128)}, f32[4096,128]{1,0:T(8,128)}, f32[4096,256]{1,0:T(8,128)}, f32[4096,256]{1,0:T(8,128)}) custom-call(bf16[32,256,256]{2,1,0:T(8,128)(2,1)} %all-to-all-done.q_ref.kv_ref, bf16[32,256,256]{2,1,0:T(8,128)(2,1)} %all-to-all-done.q_ref.kv_ref), custom_call_target="tpu_custom_call" | custom-call | flops 17179869184 | bytes 8388608 | tf_op jit(solution)/shard_map/cond/branch_0_fun/first/pallas_call | solution.py:275
  103.9 0.0 all-to-all-done.1.kv_ref
  103.9 25.4 %last_0.2 = bf16[32,128,256]{2,1,0:T(8,128)(2,1)} custom-call(bf16[32,256,256]{2,1,0:T(8,128)(2,1)} %all-to-all-done.q_ref.kv_ref, bf16[32,128,256]{2,1,0:T(8,128)(2,1)} %all-to-all-done.1.kv_ref, f32[4096,128]{1,0:T(8,128)} %get-tuple-element.30.refs_0_, f32[4096,128]{1,0:T(8,128)} %get-tuple-element.31.refs_1_, f32[4096,256]{1,0:T(8,128)} %get-tuple-element.32.refs_2_, ...), custom_call_target="tpu_custom_call" | custom-call | flops 17179869184 | bytes 8388608 | tf_op jit(solution)/shard_map/cond/branch_0_fun/last_0/pallas_call | solution.py:275
  129.3 27.2 %all_to_all.24.refs_0_ = bf16[32,128,256]{2,1,0:T(8,128)(2,1)} all-to-all(bf16[32,128,256]{2,1,0:T(8,128)(2,1)} %last_0.2), channel_id=1, replica_groups=mesh['clip'=4,'ctx'=32] {'ctx'}, dimensions={0} | all-to-all | bytes 4194304 | tf_op jit(solution)/shard_map/cond/branch_0_fun/all_to_all | solution.py:303
  156.5 2.4 %unpack.2 = (bf16[128,4096]{1,0:T(8,128)(2,1)}, bf16[128,4096]{1,0:T(8,128)(2,1)}) custom-call(bf16[32,128,256]{2,1,0:T(8,128)(2,1)} %all_to_all.24.refs_0_), custom_call_target="tpu_custom_call" | custom-call | bytes 4194304 | tf_op jit(solution)/shard_map/cond/branch_0_fun/unpack/pallas_call | solution.py:125
Async XLA Ops:
  29.1 9.7 %copy-start = (bf16[128,4096]{1,0:T(8,128)(2,1)S(1)}, bf16[128,4096]{1,0:T(8,128)(2,1)}, u32[]{:S(2)}) copy-start(bf16[128,4096]{1,0:T(8,128)(2,1)} %get-tuple-element.24.refs_0_) | copy-start | bytes 3145732 | tf_op jit(solution)/shard_map/cond
  29.1 9.7 %copy-start.2 = (bf16[128,4096]{1,0:T(8,128)(2,1)S(1)}, bf16[128,4096]{1,0:T(8,128)(2,1)}, u32[]{:S(2)}) copy-start(bf16[128,4096]{1,0:T(8,128)(2,1)} %get-tuple-element.25.refs_1_) | copy-start | bytes 3145732 | tf_op jit(solution)/shard_map/cond
  29.1 9.7 %copy-start.4 = (bf16[128,4096]{1,0:T(8,128)(2,1)S(1)}, bf16[128,4096]{1,0:T(8,128)(2,1)}, u32[]{:S(2)}) copy-start(bf16[128,4096]{1,0:T(8,128)(2,1)} %get-tuple-element.26.refs_2_) | copy-start | bytes 3145732 | tf_op jit(solution)/shard_map/cond
  29.1 42.9 %all-to-all-start = ((bf16[32,256,256]{2,1,0:T(8,128)(2,1)}), bf16[32,256,256]{2,1,0:T(8,128)(2,1)}, u32[]{:S(2)}, u32[]{:S(2)}) async-start(bf16[32,256,256]{2,1,0:T(8,128)(2,1)} %pack.4), calls=%async_computation | async-start | bytes 8388608 | tf_op jit(solution)/shard_map/cond/branch_0_fun/all_to_all | solution.py:303
  72.1 31.9 %all-to-all-start.1 = ((bf16[32,128,256]{2,1,0:T(8,128)(2,1)}), bf16[32,128,256]{2,1,0:T(8,128)(2,1)}, u32[]{:S(2)}, u32[]{:S(2)}) async-start(bf16[32,128,256]{2,1,0:T(8,128)(2,1)} %pack.5), calls=%async_computation.1 | async-start | bytes 4194304 | tf_op jit(solution)/shard_map/cond/branch_0_fun/all_to_all | solution.py:303
